TPU v7x, 128 devices: a whole 4x4x4 slice. The times are simulated.
128 devices in a mesh: samp: 32 (over y, z, core), layer: 4 (over x).
Axes of the slice: x: 4, y: 4, z: 4, core: 2. Of those that a mesh axis runs over, the one named last changes fastest.
Arguments:
- spins: int32 [256, 256], P('samp'), may hold values 0 or 1
- activations: bfloat16 [256, 8, 256, 256], P('samp', 'layer'), may hold values from -6 to 6
- cotangents: bfloat16 [256, 8, 256, 256], P('samp', 'layer'), may hold values from -0.023925781 to 0.023925781
- offdiag: float32 [256], P('samp'), may hold values from -24 to 24
Outputs:
- weights: float32 [256], P('samp')
- update: float32 [8, 256, 256], P('layer', 'samp')
All inputs are finite; a program needn't handle non-finite values. No bound on the sum of `spins` on one device may be relied on, other than what follows from the above.
Results may differ from a plain program's by a relative error of at most 0.0029.
Values may be sent and summed in bfloat16 or wider, within the bound.
A program may use at most 64 MiB of HBM per device.

v0:
```python
import jax
import jax.numpy as jnp
from jax import lax
from jax.sharding import PartitionSpec as P

SIDE = 16
shift_ratio = 0.1
highest = lax.Precision.HIGHEST


def laid_out(parts, dim):
    parts = jnp.moveaxis(parts, 0, dim)
    dims = parts.shape
    return parts.reshape(*dims[:dim], dims[dim] * dims[dim + 1], *dims[dim + 2 :])


def copy_for_each(shard, axis):
    length = lax.axis_size(axis)
    return lax.all_to_all(
        jnp.broadcast_to(shard[None], (length, *shard.shape)), axis, 0, 0, tiled=True
    )


def gather_directly(shard, axis, dim):
    return laid_out(copy_for_each(shard, axis), dim)


def local_energy(spins, offdiag):
    zvals = (2 * spins - 1).astype(jnp.float32).reshape(spins.shape[0], SIDE, SIDE)
    bonds = zvals * jnp.roll(zvals, -1, 2) + zvals * jnp.roll(zvals, -1, 1)
    return offdiag + jnp.sum(bonds, axis=(1, 2))


def small_factor(matrix):
    order = matrix.shape[0]
    positions = lax.iota(jnp.int32, order)

    def one_column(j, carry):
        rest, lower = carry
        column = lax.dynamic_slice_in_dim(rest, j, 1, 1)[:, 0]
        pivot = jnp.sqrt(lax.dynamic_slice_in_dim(column, j, 1)[0])
        scaled = jnp.where(positions >= j, column / pivot, jnp.float32(0.0))
        lower = lax.dynamic_update_slice_in_dim(lower, scaled[:, None], j, 1)
        rest = rest - scaled[:, None] * scaled[None, :]
        return (rest, lower)

    start = (matrix, jnp.zeros_like(matrix))
    return lax.fori_loop(0, order, one_column, start)[1]


def lower_inverse(lower):
    order = lower.shape[0]
    ident = jnp.eye(order, dtype=jnp.float32)

    def one_row(i, inverse):
        lower_row = lax.dynamic_slice_in_dim(lower, i, 1, 0)
        unit_row = lax.dynamic_slice_in_dim(ident, i, 1, 0)
        diag_entry = lax.dynamic_slice_in_dim(lower_row[0], i, 1)[0]
        known = jnp.dot(lower_row, inverse, precision=highest)
        fresh = (unit_row - known) / diag_entry
        return lax.dynamic_update_slice_in_dim(inverse, fresh, i, 0)

    return lax.fori_loop(0, order, one_row, jnp.zeros_like(lower))


def blocked_solve(matrix, rhs):
    block = matrix.shape[0] // 8
    lower_tiles = {}
    inverses = []
    for k in range(8):
        diag_tile = matrix[k * block : (k + 1) * block, k * block : (k + 1) * block]
        for c in range(k):
            diag_tile = diag_tile - jnp.dot(
                lower_tiles[k, c], lower_tiles[k, c].T, precision=highest
            )
        factor = small_factor(diag_tile)
        inverse = lower_inverse(factor)
        inverses.append(inverse)
        for r in range(k + 1, 8):
            tile = matrix[r * block : (r + 1) * block, k * block : (k + 1) * block]
            for c in range(k):
                tile = tile - jnp.dot(lower_tiles[r, c], lower_tiles[k, c].T, precision=highest)
            lower_tiles[r, k] = jnp.dot(tile, inverse.T, precision=highest)
    forward = []
    for k in range(8):
        piece = rhs[k * block : (k + 1) * block]
        for c in range(k):
            piece = piece - jnp.dot(lower_tiles[k, c], forward[c], precision=highest)
        forward.append(jnp.dot(inverses[k], piece, precision=highest))
    backward = [None] * 8
    for k in range(7, -1, -1):
        piece = forward[k]
        for r in range(k + 1, 8):
            piece = piece - jnp.dot(lower_tiles[r, k].T, backward[r], precision=highest)
        backward[k] = jnp.dot(inverses[k].T, piece, precision=highest)
    return jnp.concatenate(backward)


def body(spins, activations, cotangents, offdiag):
    s_local = spins.shape[0]
    energy_local = local_energy(spins, offdiag)
    energy = gather_directly(energy_local, "samp", 0)
    total = energy.shape[0]
    eps = (energy - jnp.mean(energy)) / jnp.sqrt(jnp.float32(total))
    jac = jnp.einsum(
        "ksad,ksae->ksde", activations, cotangents, preferred_element_type=jnp.float32
    ).astype(jnp.bfloat16)
    regrouped = lax.all_to_all(jac, "samp", split_axis=2, concat_axis=0, tiled=True)
    flat = regrouped.reshape(total, -1)
    col_mean = jnp.mean(flat, axis=0, dtype=jnp.float32)
    raw_gram = jnp.dot(flat, flat.T, preferred_element_type=jnp.float32)
    row_dots = jnp.dot(flat.astype(jnp.float32), col_mean, precision=highest)
    mean_square = jnp.sum(col_mean * col_mean)
    partial_value = (raw_gram - row_dots[:, None] - row_dots[None, :] + mean_square) / total
    gram = lax.psum(partial_value, ("samp", "layer"))
    shift = shift_ratio * jnp.trace(gram) / total
    weights = blocked_solve(gram + shift * jnp.eye(total, dtype=jnp.float32), eps)
    start = lax.axis_index("samp") * s_local
    own_weights = lax.dynamic_slice_in_dim(weights, start, s_local)
    coeffs_all = weights - jnp.mean(weights)
    update = jnp.dot(coeffs_all, flat.astype(jnp.float32), precision=highest).reshape(
        regrouped.shape[1:]
    )
    return (own_weights, update)


def solution(mesh):
    placed = (
        P("samp", None),
        P("samp", "layer", None, None),
        P("samp", "layer", None, None),
        P("samp"),
    )
    return jax.shard_map(
        body,
        mesh=mesh,
        in_specs=placed,
        out_specs=(P("samp"), P("layer", "samp", None)),
        check_vma=False,
    )
```

profile of v0, /device:TPU:1, one launch (start us, length us, event | category | flops | bytes accessed | tf_op | source)
XLA Modules:
  0.0 995.8 jit_solution(18253489442866644126)
XLA Ops:
  7.2 0.9 add_convert_fusion
  8.4 0.8 multiply_reduce_fusion.1
  10.5 9.6 all-to-all-start.1
  20.1 2.4 convolution_convert_fusion
  22.5 3.5 copy.85
  25.9 1.0 all-to-all-done.1
  27.0 6.4 all-to-all-start
  34.7 27.0 %all-to-all-done = bf16[8,2,256,256]{3,1,0,2:T(2,128)(2,1)} async-done(((bf16[8,2,256,256]{3,1,0,2:T(2,128)(2,1)}), bf16[8,2,256,256]{3,1,0,2:T(2,128)(2,1)}, u32[]{:S(2)}, u32[]{:S(2)}) %all-to-all-start) | async-done | bytes 2097184 | tf_op jit(solution)/shard_map/all_to_all | solution.py:108
  61.7 2.8 convert_reduce_fusion
  64.5 4.2 copy.135
  68.8 4.2 reshape.493
  73.6 3.5 fusion.238
  77.1 2.1 fusion.52
  79.9 3.6 copy.128
  83.5 134.9 %all-reduce.2.cloned.1.call-done = f32[256,256]{1,0:T(8,128)} async-done(((f32[256,256]{1,0:T(8,128)}), f32[256,256]{1,0:T(8,128)}) %all-reduce.2.cloned.1.call-update) | async-done | bytes 262160 | tf_op jit(solution)/shard_map/psum | solution.py:115
  218.4 1.6 select_reduce_fusion
  220.6 1.0 select_add_fusion
  221.7 44.8 %while.288 = (s32[]{:T(128)}, f32[32,32]{0,1:T(8,128)S(1)}, f32[32,32]{0,1:T(8,128)S(1)}, s32[]{:T(128)}, s32[]{:T(128)}, /*index=5*/s32[]{:T(128)}) while((s32[]{:T(128)}, f32[32,32]{0,1:T(8,128)S(1)}, f32[32,32]{0,1:T(8,128)S(1)}, s32[]{:T(128)}, s32[]{:T(128)}, /*index=5*/s32[]{:T(128)}) %tuple.681), condition=%wide.region_5.6_spmd.clone, body=%wide.region_4.5_spmd.clone.sunk | while | flops 2211 | bytes 10493 | solution.py:48
  266.6 45.1 %while.280 = (s32[]{:T(128)}, f32[32,32]{1,0:T(8,128)S(1)}, f32[32,32]{1,0:T(8,128)S(1)}, f32[32,32]{1,0:T(8,128)S(1)}, s32[]{:T(128)}, /*index=5*/s32[]{:T(128)}, s32[]{:T(128)}) while((s32[]{:T(128)}, f32[32,32]{1,0:T(8,128)S(1)}, f32[32,32]{1,0:T(8,128)S(1)}, f32[32,32]{1,0:T(8,128)S(1)}, s32[]{:T(128)}, /*index=5*/s32[]{:T(128)}, ...), condition=%wide.region_7.8_spmd, body=%wide.region_6.7_spmd.sunk | while | flops 12355 | bytes 18937 | solution.py:63
  268.6 0.8 fusion.577
  270.0 0.8 fusion.577
  272.8 0.8 fusion.577
  274.2 0.8 fusion.577
  277.0 0.8 fusion.577
  279.9 0.8 fusion.577
  281.3 0.8 fusion.577
  284.1 0.8 fusion.577
  285.5 0.8 fusion.577
  288.3 0.8 fusion.577
  289.7 0.8 fusion.577
  291.1 0.8 fusion.577
  292.5 0.8 fusion.577
  318.4 45.6 %while.289 = (s32[]{:T(128)}, f32[32,32]{0,1:T(8,128)S(1)}, f32[32,32]{0,1:T(8,128)S(1)}, s32[]{:T(128)}, s32[]{:T(128)}, /*index=5*/s32[]{:T(128)}) while((s32[]{:T(128)}, f32[32,32]{0,1:T(8,128)S(1)}, f32[32,32]{0,1:T(8,128)S(1)}, s32[]{:T(128)}, s32[]{:T(128)}, /*index=5*/s32[]{:T(128)}) %tuple.687), condition=%wide.region_11.12_spmd.clone, body=%wide.region_10.11_spmd.clone.sunk | while | flops 2211 | bytes 10493 | solution.py:48
  364.0 45.1 %while.281 = (s32[]{:T(128)}, f32[32,32]{1,0:T(8,128)S(1)}, f32[32,32]{1,0:T(8,128)S(1)}, f32[32,32]{1,0:T(8,128)S(1)}, s32[]{:T(128)}, /*index=5*/s32[]{:T(128)}, s32[]{:T(128)}) while((s32[]{:T(128)}, f32[32,32]{1,0:T(8,128)S(1)}, f32[32,32]{1,0:T(8,128)S(1)}, f32[32,32]{1,0:T(8,128)S(1)}, s32[]{:T(128)}, /*index=5*/s32[]{:T(128)}, ...), condition=%wide.region_13.14_spmd, body=%wide.region_12.13_spmd.sunk | while | flops 12355 | bytes 18937 | solution.py:63
  412.9 45.5 %while.290 = (s32[]{:T(128)}, f32[32,32]{0,1:T(8,128)S(1)}, f32[32,32]{0,1:T(8,128)S(1)}, s32[]{:T(128)}, s32[]{:T(128)}, /*index=5*/s32[]{:T(128)}) while((s32[]{:T(128)}, f32[32,32]{0,1:T(8,128)S(1)}, f32[32,32]{0,1:T(8,128)S(1)}, s32[]{:T(128)}, s32[]{:T(128)}, /*index=5*/s32[]{:T(128)}) %tuple.693), condition=%wide.region_15.16_spmd.clone, body=%wide.region_14.15_spmd.clone.sunk | while | flops 2211 | bytes 10493 | solution.py:48
  458.5 45.1 %while.282 = (s32[]{:T(128)}, f32[32,32]{1,0:T(8,128)S(1)}, f32[32,32]{1,0:T(8,128)S(1)}, f32[32,32]{1,0:T(8,128)S(1)}, s32[]{:T(128)}, /*index=5*/s32[]{:T(128)}, s32[]{:T(128)}) while((s32[]{:T(128)}, f32[32,32]{1,0:T(8,128)S(1)}, f32[32,32]{1,0:T(8,128)S(1)}, f32[32,32]{1,0:T(8,128)S(1)}, s32[]{:T(128)}, /*index=5*/s32[]{:T(128)}, ...), condition=%wide.region_17.18_spmd, body=%wide.region_16.17_spmd.sunk | while | flops 12355 | bytes 18937 | solution.py:63
  507.4 45.5 %while.291 = (s32[]{:T(128)}, f32[32,32]{0,1:T(8,128)S(1)}, f32[32,32]{0,1:T(8,128)S(1)}, s32[]{:T(128)}, s32[]{:T(128)}, /*index=5*/s32[]{:T(128)}) while((s32[]{:T(128)}, f32[32,32]{0,1:T(8,128)S(1)}, f32[32,32]{0,1:T(8,128)S(1)}, s32[]{:T(128)}, s32[]{:T(128)}, /*index=5*/s32[]{:T(128)}) %tuple.699), condition=%wide.region_19.20_spmd.clone, body=%wide.region_18.19_spmd.clone.sunk | while | flops 2211 | bytes 10493 | solution.py:48
  553.0 45.1 %while.283 = (s32[]{:T(128)}, f32[32,32]{1,0:T(8,128)S(1)}, f32[32,32]{1,0:T(8,128)S(1)}, f32[32,32]{1,0:T(8,128)S(1)}, s32[]{:T(128)}, /*index=5*/s32[]{:T(128)}, s32[]{:T(128)}) while((s32[]{:T(128)}, f32[32,32]{1,0:T(8,128)S(1)}, f32[32,32]{1,0:T(8,128)S(1)}, f32[32,32]{1,0:T(8,128)S(1)}, s32[]{:T(128)}, /*index=5*/s32[]{:T(128)}, ...), condition=%wide.region_21.22_spmd, body=%wide.region_20.21_spmd.sunk | while | flops 12355 | bytes 18937 | solution.py:63
  601.6 45.5 %while.292 = (s32[]{:T(128)}, f32[32,32]{0,1:T(8,128)S(1)}, f32[32,32]{0,1:T(8,128)S(1)}, s32[]{:T(128)}, s32[]{:T(128)}, /*index=5*/s32[]{:T(128)}) while((s32[]{:T(128)}, f32[32,32]{0,1:T(8,128)S(1)}, f32[32,32]{0,1:T(8,128)S(1)}, s32[]{:T(128)}, s32[]{:T(128)}, /*index=5*/s32[]{:T(128)}) %tuple.705), condition=%wide.region_23.24_spmd.clone, body=%wide.region_22.23_spmd.clone.sunk | while | flops 2211 | bytes 10493 | solution.py:48
  647.2 45.1 %while.284 = (s32[]{:T(128)}, f32[32,32]{1,0:T(8,128)S(1)}, f32[32,32]{1,0:T(8,128)S(1)}, f32[32,32]{1,0:T(8,128)S(1)}, s32[]{:T(128)}, /*index=5*/s32[]{:T(128)}, s32[]{:T(128)}) while((s32[]{:T(128)}, f32[32,32]{1,0:T(8,128)S(1)}, f32[32,32]{1,0:T(8,128)S(1)}, f32[32,32]{1,0:T(8,128)S(1)}, s32[]{:T(128)}, /*index=5*/s32[]{:T(128)}, ...), condition=%wide.region_25.26_spmd, body=%wide.region_24.25_spmd.sunk | while | flops 12355 | bytes 18937 | solution.py:63
  695.8 45.5 %while.293 = (s32[]{:T(128)}, f32[32,32]{0,1:T(8,128)S(1)}, f32[32,32]{0,1:T(8,128)S(1)}, s32[]{:T(128)}, s32[]{:T(128)}, /*index=5*/s32[]{:T(128)}) while((s32[]{:T(128)}, f32[32,32]{0,1:T(8,128)S(1)}, f32[32,32]{0,1:T(8,128)S(1)}, s32[]{:T(128)}, s32[]{:T(128)}, /*index=5*/s32[]{:T(128)}) %tuple.711), condition=%wide.region_27.28_spmd.clone, body=%wide.region_26.27_spmd.clone.sunk | while | flops 2211 | bytes 10493 | solution.py:48
  741.4 45.1 %while.285 = (s32[]{:T(128)}, f32[32,32]{1,0:T(8,128)S(1)}, f32[32,32]{1,0:T(8,128)S(1)}, f32[32,32]{1,0:T(8,128)S(1)}, s32[]{:T(128)}, /*index=5*/s32[]{:T(128)}, s32[]{:T(128)}) while((s32[]{:T(128)}, f32[32,32]{1,0:T(8,128)S(1)}, f32[32,32]{1,0:T(8,128)S(1)}, f32[32,32]{1,0:T(8,128)S(1)}, s32[]{:T(128)}, /*index=5*/s32[]{:T(128)}, ...), condition=%wide.region_29.30_spmd, body=%wide.region_28.29_spmd.sunk | while | flops 12355 | bytes 18937 | solution.py:63
  787.8 45.5 %while.294 = (s32[]{:T(128)}, f32[32,32]{0,1:T(8,128)S(1)}, f32[32,32]{0,1:T(8,128)S(1)}, s32[]{:T(128)}, s32[]{:T(128)}, /*index=5*/s32[]{:T(128)}) while((s32[]{:T(128)}, f32[32,32]{0,1:T(8,128)S(1)}, f32[32,32]{0,1:T(8,128)S(1)}, s32[]{:T(128)}, s32[]{:T(128)}, /*index=5*/s32[]{:T(128)}) %tuple.717), condition=%wide.region_31.32_spmd.clone, body=%wide.region_30.31_spmd.clone.sunk | while | flops 2211 | bytes 10493 | solution.py:48
  833.4 45.1 %while.286 = (s32[]{:T(128)}, f32[32,32]{1,0:T(8,128)S(1)}, f32[32,32]{1,0:T(8,128)S(1)}, f32[32,32]{1,0:T(8,128)S(1)}, s32[]{:T(128)}, /*index=5*/s32[]{:T(128)}, s32[]{:T(128)}) while((s32[]{:T(128)}, f32[32,32]{1,0:T(8,128)S(1)}, f32[32,32]{1,0:T(8,128)S(1)}, f32[32,32]{1,0:T(8,128)S(1)}, s32[]{:T(128)}, /*index=5*/s32[]{:T(128)}, ...), condition=%wide.region_33.34_spmd, body=%wide.region_32.33_spmd.sunk | while | flops 12355 | bytes 18937 | solution.py:63
  879.0 45.5 %while.295 = (s32[]{:T(128)}, f32[32,32]{0,1:T(8,128)S(1)}, f32[32,32]{0,1:T(8,128)S(1)}, s32[]{:T(128)}, s32[]{:T(128)}, /*index=5*/s32[]{:T(128)}) while((s32[]{:T(128)}, f32[32,32]{0,1:T(8,128)S(1)}, f32[32,32]{0,1:T(8,128)S(1)}, s32[]{:T(128)}, s32[]{:T(128)}, /*index=5*/s32[]{:T(128)}) %tuple.723), condition=%wide.region_35.36_spmd.clone, body=%wide.region_34.35_spmd.clone.sunk | while | flops 2211 | bytes 10493 | solution.py:48
  924.6 45.1 %while.287 = (s32[]{:T(128)}, f32[32,32]{1,0:T(8,128)S(1)}, f32[32,32]{1,0:T(8,128)S(1)}, f32[32,32]{1,0:T(8,128)S(1)}, s32[]{:T(128)}, /*index=5*/s32[]{:T(128)}, s32[]{:T(128)}) while((s32[]{:T(128)}, f32[32,32]{1,0:T(8,128)S(1)}, f32[32,32]{1,0:T(8,128)S(1)}, f32[32,32]{1,0:T(8,128)S(1)}, s32[]{:T(128)}, /*index=5*/s32[]{:T(128)}, ...), condition=%wide.region_37.38_spmd, body=%wide.region_36.37_spmd.sunk | while | flops 12355 | bytes 18937 | solution.py:63
  977.4 0.8 bitcast_reduce_fusion
  985.5 2.8 fusion.48
  (2283 shorter events, 565.0 us)
Async XLA Ops:
  7.2 13.0 %copy-start = (bf16[8,2,256,256]{3,2,1,0:T(8,128)(2,1)S(1)}, bf16[8,2,256,256]{3,2,1,0:T(8,128)(2,1)}, u32[]{:S(2)}) copy-start(bf16[8,2,256,256]{3,2,1,0:T(8,128)(2,1)} %param.37) | copy-start | bytes 6291460
  10.5 16.5 %all-to-all-start.1 = ((f32[32,1,8]{2,1,0:T(1,128)}), f32[32,1,8]{2,1,0:T(1,128)S(1)}, u32[]{:S(2)}, u32[]{:S(2)}) async-start(f32[32,1,8]{2,1,0:T(1,128)} %broadcast_in_dim.126), calls=%async_computation.1 | async-start | bytes 32768 | tf_op jit(solution)/shard_map/all_to_all | solution.py:19
  27.0 34.8 %all-to-all-start = ((bf16[8,2,256,256]{3,1,0,2:T(2,128)(2,1)}), bf16[8,2,256,256]{3,1,0,2:T(2,128)(2,1)}, u32[]{:S(2)}, u32[]{:S(2)}) async-start(bf16[8,2,256,256]{3,1,0,2:T(2,128)(2,1)} %copy.85), calls=%async_computation | async-start | bytes 4194304 | tf_op jit(solution)/shard_map/all_to_all | solution.py:108
  33.4 185.0 %all-reduce.2.cloned.1.call-start = ((), (), s32[]{:S(2)}) async-start(), calls=%async_computation.2 | async-start | bytes 524288 | tf_op jit(solution)/shard_map/psum | solution.py:115
  73.6 3.5 copy-start.1
Sparse Core Ops, SparseCore 0:
  79.3 139.0 all-reduce.1
where the time goes:
time: 1000 us; the launch traced here: 996 us
  local copies, waits for them, and re-layouts  334 us (33%)
  matrix products  242 us (24%)
  loops' own time  186 us (19%)
  waiting for transfers between devices  163 us (16%)
  other arithmetic  32.5 us (3%)
  between operations  21.3 us (2%)
  starting transfers between devices  16 us (2%)
    dot_general x256, matrix products, one_row(): known = jnp.dot(lower_row, inverse, precision=highest)  200 us
    another operation x8, loops' own time, small_factor(): return lax.fori_loop(0, order, one_column, start)[1]  183 us
    dynamic_slice x256, local copies, waits for them, and re-layouts, one_column(): pivot = jnp.sqrt(lax.dynamic_slice_in_dim(column, j, 1)[0])  151 us
    dynamic_slice x256, local copies, waits for them, and re-layouts, one_row(): diag_entry = lax.dynamic_slice_in_dim(lower_row[0], i, 1)[0]  151 us
    psum x1, waiting for transfers between devices, body(): gram = lax.psum(partial_value, ('samp', 'layer'))  135 us
    all_to_all x1, waiting for transfers between devices, body(): lax.all_to_all(jac, 'samp', split_axis=2, concat_axis=0, tiled=True)  27 us
  transfers between devices with their start and end apart: 3, of which 3 were waited for; matrix products, arithmetic and copies ran while one was open for 1% of the time, Pallas kernels for 0%

commit v1 on v0

--- a/solution.py
+++ b/solution.py
@@ -112,7 +112,7 @@
     row_dots = jnp.dot(flat.astype(jnp.float32), col_mean, precision=highest)
     mean_square = jnp.sum(col_mean * col_mean)
     partial_value = (raw_gram - row_dots[:, None] - row_dots[None, :] + mean_square) / total
-    gram = lax.psum(partial_value, ("samp", "layer"))
+    gram = lax.psum(lax.psum(partial_value, "samp"), "layer")
     shift = shift_ratio * jnp.trace(gram) / total
     weights = blocked_solve(gram + shift * jnp.eye(total, dtype=jnp.float32), eps)
     start = lax.axis_index("samp") * s_local

time: 1000 us -> 996 us (level)
    psum x1 -> x2, waiting for transfers between devices: 135 us -> 123 us  [body(): gram = lax.psum(lax.psum(partial_value, 'samp'), 'layer')]
  transfers between devices with their start and end apart: 3 -> 4, of which waited for: 3 -> 4; matrix products, arithmetic and copies ran while one was open for 1% -> 1% of each run, Pallas kernels for 0% -> 0%
where the time goes in v1:
time: 996 us; the launch traced here: 989 us
  local copies, waits for them, and re-layouts  336 us (34%)
  matrix products  242 us (24%)
  loops' own time  187 us (19%)
  waiting for transfers between devices  158 us (16%)
  other arithmetic  30.3 us (3%)
  between operations  21.4 us (2%)
  starting transfers between devices  14.4 us (1%)
    dot_general x256, matrix products, one_row(): known = jnp.dot(lower_row, inverse, precision=highest)  200 us
    another operation x8, loops' own time, small_factor(): return lax.fori_loop(0, order, one_column, start)[1]  184 us
    dynamic_slice x256, local copies, waits for them, and re-layouts, one_column(): pivot = jnp.sqrt(lax.dynamic_slice_in_dim(column, j, 1)[0])  151 us
    dynamic_slice x256, local copies, waits for them, and re-layouts, one_row(): diag_entry = lax.dynamic_slice_in_dim(lower_row[0], i, 1)[0]  151 us
    psum x2, waiting for transfers between devices, body(): gram = lax.psum(lax.psum(partial_value, 'samp'), 'layer')  123 us
    all_to_all x1, waiting for transfers between devices, body(): lax.all_to_all(jac, 'samp', split_axis=2, concat_axis=0, tiled=True)  27.9 us
  transfers between devices with their start and end apart: 4, of which 4 were waited for; matrix products, arithmetic and copies ran while one was open for 1% of the time, Pallas kernels for 0%

profile of v1, /device:TPU:1, one launch (start us, length us, event | category | flops | bytes accessed | tf_op | source)
XLA Modules:
  0.0 989.1 jit_solution(8808383684421962730)
XLA Ops:
  7.2 1.6 copy-done
  8.8 2.4 convolution_convert_fusion
  11.1 3.5 copy.85
  14.6 9.8 all-to-all-start
  24.8 27.9 %all-to-all-done = bf16[8,2,256,256]{3,1,0,2:T(2,128)(2,1)} async-done(((bf16[8,2,256,256]{3,1,0,2:T(2,128)(2,1)}), bf16[8,2,256,256]{3,1,0,2:T(2,128)(2,1)}, u32[]{:S(2)}, u32[]{:S(2)}) %all-to-all-start) | async-done | bytes 2097184 | tf_op jit(solution)/shard_map/all_to_all | solution.py:108
  52.7 2.8 convert_reduce_fusion
  55.5 4.2 copy.135
  59.8 4.2 reshape.493
  64.6 3.5 fusion.238
  68.1 2.1 fusion.52
  71.0 4.3 all-to-all-start.1
  75.6 6.7 all-to-all-done.1
  83.6 86.0 %all-reduce.3.cloned.1.call-done = f32[256,256]{1,0:T(8,128)} async-done(((f32[256,256]{1,0:T(8,128)}), f32[256,256]{1,0:T(8,128)}) %all-reduce.3.cloned.1.call-update) | async-done | bytes 262160 | tf_op jit(solution)/shard_map/psum | solution.py:115
  170.4 3.6 copy.128
  174.0 37.0 %all-reduce.5.cloned.1.call-done = f32[256,256]{1,0:T(8,128)} async-done(((f32[256,256]{1,0:T(8,128)}), f32[256,256]{1,0:T(8,128)}) %all-reduce.5.cloned.1.call-update) | async-done | bytes 262160 | tf_op jit(solution)/shard_map/psum | solution.py:115
  211.0 1.6 select_reduce_fusion
  213.2 1.0 select_add_fusion
  214.3 45.5 %while.288 = (s32[]{:T(128)}, f32[32,32]{0,1:T(8,128)S(1)}, f32[32,32]{0,1:T(8,128)S(1)}, s32[]{:T(128)}, s32[]{:T(128)}, /*index=5*/s32[]{:T(128)}) while((s32[]{:T(128)}, f32[32,32]{0,1:T(8,128)S(1)}, f32[32,32]{0,1:T(8,128)S(1)}, s32[]{:T(128)}, s32[]{:T(128)}, /*index=5*/s32[]{:T(128)}) %tuple.681), condition=%wide.region_6.7_spmd.clone, body=%wide.region_5.6_spmd.clone.sunk | while | flops 2211 | bytes 10493 | solution.py:48
  259.9 45.1 %while.280 = (s32[]{:T(128)}, f32[32,32]{1,0:T(8,128)S(1)}, f32[32,32]{1,0:T(8,128)S(1)}, f32[32,32]{1,0:T(8,128)S(1)}, s32[]{:T(128)}, /*index=5*/s32[]{:T(128)}, s32[]{:T(128)}) while((s32[]{:T(128)}, f32[32,32]{1,0:T(8,128)S(1)}, f32[32,32]{1,0:T(8,128)S(1)}, f32[32,32]{1,0:T(8,128)S(1)}, s32[]{:T(128)}, /*index=5*/s32[]{:T(128)}, ...), condition=%wide.region_8.9_spmd, body=%wide.region_7.8_spmd.sunk | while | flops 12355 | bytes 18937 | solution.py:63
  260.5 0.8 fusion.577
  261.9 0.8 fusion.577
  263.3 0.8 fusion.577
  264.7 0.8 fusion.577
  267.5 0.8 fusion.577
  268.9 0.8 fusion.577
  271.8 0.8 fusion.577
  273.2 0.8 fusion.577
  276.0 0.8 fusion.577
  278.8 0.8 fusion.577
  280.2 0.8 fusion.577
  283.0 0.8 fusion.577
  284.4 0.8 fusion.577
  311.7 45.6 %while.289 = (s32[]{:T(128)}, f32[32,32]{0,1:T(8,128)S(1)}, f32[32,32]{0,1:T(8,128)S(1)}, s32[]{:T(128)}, s32[]{:T(128)}, /*index=5*/s32[]{:T(128)}) while((s32[]{:T(128)}, f32[32,32]{0,1:T(8,128)S(1)}, f32[32,32]{0,1:T(8,128)S(1)}, s32[]{:T(128)}, s32[]{:T(128)}, /*index=5*/s32[]{:T(128)}) %tuple.687), condition=%wide.region_12.13_spmd.clone, body=%wide.region_11.12_spmd.clone.sunk | while | flops 2211 | bytes 10493 | solution.py:48
  357.4 45.1 %while.281 = (s32[]{:T(128)}, f32[32,32]{1,0:T(8,128)S(1)}, f32[32,32]{1,0:T(8,128)S(1)}, f32[32,32]{1,0:T(8,128)S(1)}, s32[]{:T(128)}, /*index=5*/s32[]{:T(128)}, s32[]{:T(128)}) while((s32[]{:T(128)}, f32[32,32]{1,0:T(8,128)S(1)}, f32[32,32]{1,0:T(8,128)S(1)}, f32[32,32]{1,0:T(8,128)S(1)}, s32[]{:T(128)}, /*index=5*/s32[]{:T(128)}, ...), condition=%wide.region_14.15_spmd, body=%wide.region_13.14_spmd.sunk | while | flops 12355 | bytes 18937 | solution.py:63
  406.2 45.5 %while.290 = (s32[]{:T(128)}, f32[32,32]{0,1:T(8,128)S(1)}, f32[32,32]{0,1:T(8,128)S(1)}, s32[]{:T(128)}, s32[]{:T(128)}, /*index=5*/s32[]{:T(128)}) while((s32[]{:T(128)}, f32[32,32]{0,1:T(8,128)S(1)}, f32[32,32]{0,1:T(8,128)S(1)}, s32[]{:T(128)}, s32[]{:T(128)}, /*index=5*/s32[]{:T(128)}) %tuple.693), condition=%wide.region_16.17_spmd.clone, body=%wide.region_15.16_spmd.clone.sunk | while | flops 2211 | bytes 10493 | solution.py:48
  451.8 45.1 %while.282 = (s32[]{:T(128)}, f32[32,32]{1,0:T(8,128)S(1)}, f32[32,32]{1,0:T(8,128)S(1)}, f32[32,32]{1,0:T(8,128)S(1)}, s32[]{:T(128)}, /*index=5*/s32[]{:T(128)}, s32[]{:T(128)}) while((s32[]{:T(128)}, f32[32,32]{1,0:T(8,128)S(1)}, f32[32,32]{1,0:T(8,128)S(1)}, f32[32,32]{1,0:T(8,128)S(1)}, s32[]{:T(128)}, /*index=5*/s32[]{:T(128)}, ...), condition=%wide.region_18.19_spmd, body=%wide.region_17.18_spmd.sunk | while | flops 12355 | bytes 18937 | solution.py:63
  500.7 45.5 %while.291 = (s32[]{:T(128)}, f32[32,32]{0,1:T(8,128)S(1)}, f32[32,32]{0,1:T(8,128)S(1)}, s32[]{:T(128)}, s32[]{:T(128)}, /*index=5*/s32[]{:T(128)}) while((s32[]{:T(128)}, f32[32,32]{0,1:T(8,128)S(1)}, f32[32,32]{0,1:T(8,128)S(1)}, s32[]{:T(128)}, s32[]{:T(128)}, /*index=5*/s32[]{:T(128)}) %tuple.699), condition=%wide.region_20.21_spmd.clone, body=%wide.region_19.20_spmd.clone.sunk | while | flops 2211 | bytes 10493 | solution.py:48
  546.3 45.1 %while.283 = (s32[]{:T(128)}, f32[32,32]{1,0:T(8,128)S(1)}, f32[32,32]{1,0:T(8,128)S(1)}, f32[32,32]{1,0:T(8,128)S(1)}, s32[]{:T(128)}, /*index=5*/s32[]{:T(128)}, s32[]{:T(128)}) while((s32[]{:T(128)}, f32[32,32]{1,0:T(8,128)S(1)}, f32[32,32]{1,0:T(8,128)S(1)}, f32[32,32]{1,0:T(8,128)S(1)}, s32[]{:T(128)}, /*index=5*/s32[]{:T(128)}, ...), condition=%wide.region_22.23_spmd, body=%wide.region_21.22_spmd.sunk | while | flops 12355 | bytes 18937 | solution.py:63
  594.9 45.5 %while.292 = (s32[]{:T(128)}, f32[32,32]{0,1:T(8,128)S(1)}, f32[32,32]{0,1:T(8,128)S(1)}, s32[]{:T(128)}, s32[]{:T(128)}, /*index=5*/s32[]{:T(128)}) while((s32[]{:T(128)}, f32[32,32]{0,1:T(8,128)S(1)}, f32[32,32]{0,1:T(8,128)S(1)}, s32[]{:T(128)}, s32[]{:T(128)}, /*index=5*/s32[]{:T(128)}) %tuple.705), condition=%wide.region_24.25_spmd.clone, body=%wide.region_23.24_spmd.clone.sunk | while | flops 2211 | bytes 10493 | solution.py:48
  640.5 45.1 %while.284 = (s32[]{:T(128)}, f32[32,32]{1,0:T(8,128)S(1)}, f32[32,32]{1,0:T(8,128)S(1)}, f32[32,32]{1,0:T(8,128)S(1)}, s32[]{:T(128)}, /*index=5*/s32[]{:T(128)}, s32[]{:T(128)}) while((s32[]{:T(128)}, f32[32,32]{1,0:T(8,128)S(1)}, f32[32,32]{1,0:T(8,128)S(1)}, f32[32,32]{1,0:T(8,128)S(1)}, s32[]{:T(128)}, /*index=5*/s32[]{:T(128)}, ...), condition=%wide.region_26.27_spmd, body=%wide.region_25.26_spmd.sunk | while | flops 12355 | bytes 18937 | solution.py:63
  689.1 45.5 %while.293 = (s32[]{:T(128)}, f32[32,32]{0,1:T(8,128)S(1)}, f32[32,32]{0,1:T(8,128)S(1)}, s32[]{:T(128)}, s32[]{:T(128)}, /*index=5*/s32[]{:T(128)}) while((s32[]{:T(128)}, f32[32,32]{0,1:T(8,128)S(1)}, f32[32,32]{0,1:T(8,128)S(1)}, s32[]{:T(128)}, s32[]{:T(128)}, /*index=5*/s32[]{:T(128)}) %tuple.711), condition=%wide.region_28.29_spmd.clone, body=%wide.region_27.28_spmd.clone.sunk | while | flops 2211 | bytes 10493 | solution.py:48
  734.7 45.1 %while.285 = (s32[]{:T(128)}, f32[32,32]{1,0:T(8,128)S(1)}, f32[32,32]{1,0:T(8,128)S(1)}, f32[32,32]{1,0:T(8,128)S(1)}, s32[]{:T(128)}, /*index=5*/s32[]{:T(128)}, s32[]{:T(128)}) while((s32[]{:T(128)}, f32[32,32]{1,0:T(8,128)S(1)}, f32[32,32]{1,0:T(8,128)S(1)}, f32[32,32]{1,0:T(8,128)S(1)}, s32[]{:T(128)}, /*index=5*/s32[]{:T(128)}, ...), condition=%wide.region_30.31_spmd, body=%wide.region_29.30_spmd.sunk | while | flops 12355 | bytes 18937 | solution.py:63
  781.1 45.5 %while.294 = (s32[]{:T(128)}, f32[32,32]{0,1:T(8,128)S(1)}, f32[32,32]{0,1:T(8,128)S(1)}, s32[]{:T(128)}, s32[]{:T(128)}, /*index=5*/s32[]{:T(128)}) while((s32[]{:T(128)}, f32[32,32]{0,1:T(8,128)S(1)}, f32[32,32]{0,1:T(8,128)S(1)}, s32[]{:T(128)}, s32[]{:T(128)}, /*index=5*/s32[]{:T(128)}) %tuple.717), condition=%wide.region_32.33_spmd.clone, body=%wide.region_31.32_spmd.clone.sunk | while | flops 2211 | bytes 10493 | solution.py:48
  826.7 45.1 %while.286 = (s32[]{:T(128)}, f32[32,32]{1,0:T(8,128)S(1)}, f32[32,32]{1,0:T(8,128)S(1)}, f32[32,32]{1,0:T(8,128)S(1)}, s32[]{:T(128)}, /*index=5*/s32[]{:T(128)}, s32[]{:T(128)}) while((s32[]{:T(128)}, f32[32,32]{1,0:T(8,128)S(1)}, f32[32,32]{1,0:T(8,128)S(1)}, f32[32,32]{1,0:T(8,128)S(1)}, s32[]{:T(128)}, /*index=5*/s32[]{:T(128)}, ...), condition=%wide.region_34.35_spmd, body=%wide.region_33.34_spmd.sunk | while | flops 12355 | bytes 18937 | solution.py:63
  872.3 45.5 %while.295 = (s32[]{:T(128)}, f32[32,32]{0,1:T(8,128)S(1)}, f32[32,32]{0,1:T(8,128)S(1)}, s32[]{:T(128)}, s32[]{:T(128)}, /*index=5*/s32[]{:T(128)}) while((s32[]{:T(128)}, f32[32,32]{0,1:T(8,128)S(1)}, f32[32,32]{0,1:T(8,128)S(1)}, s32[]{:T(128)}, s32[]{:T(128)}, /*index=5*/s32[]{:T(128)}) %tuple.723), condition=%wide.region_36.37_spmd.clone, body=%wide.region_35.36_spmd.clone.sunk | while | flops 2211 | bytes 10493 | solution.py:48
  918.0 45.1 %while.287 = (s32[]{:T(128)}, f32[32,32]{1,0:T(8,128)S(1)}, f32[32,32]{1,0:T(8,128)S(1)}, f32[32,32]{1,0:T(8,128)S(1)}, s32[]{:T(128)}, /*index=5*/s32[]{:T(128)}, s32[]{:T(128)}) while((s32[]{:T(128)}, f32[32,32]{1,0:T(8,128)S(1)}, f32[32,32]{1,0:T(8,128)S(1)}, f32[32,32]{1,0:T(8,128)S(1)}, s32[]{:T(128)}, /*index=5*/s32[]{:T(128)}, ...), condition=%wide.region_38.39_spmd, body=%wide.region_37.38_spmd.sunk | while | flops 12355 | bytes 18937 | solution.py:63
  970.7 0.8 bitcast_reduce_fusion
  978.8 2.8 fusion.48
  (2290 shorter events, 564.4 us)
Async XLA Ops:
  7.2 1.6 copy-start
  14.6 9.8 copy-start.2
  14.6 38.1 %all-to-all-start = ((bf16[8,2,256,256]{3,1,0,2:T(2,128)(2,1)}), bf16[8,2,256,256]{3,1,0,2:T(2,128)(2,1)}, u32[]{:S(2)}, u32[]{:S(2)}) async-start(bf16[8,2,256,256]{3,1,0,2:T(2,128)(2,1)} %copy.85), calls=%async_computation | async-start | bytes 4194304 | tf_op jit(solution)/shard_map/all_to_all | solution.py:108
  24.4 145.2 %all-reduce.3.cloned.1.call-start = ((), (), s32[]{:S(2)}) async-start(), calls=%async_computation.2 | async-start | bytes 524288 | tf_op jit(solution)/shard_map/psum | solution.py:115
  64.6 3.5 copy-start.1
  68.1 2.3 copy-start.3
  71.0 11.3 %all-to-all-start.1 = ((f32[32,1,8]{2,1,0:T(1,128)}), f32[32,1,8]{2,1,0:T(1,128)S(1)}, u32[]{:S(2)}, u32[]{:S(2)}) async-start(f32[32,1,8]{2,1,0:T(1,128)} %broadcast_in_dim.126), calls=%async_computation.1 | async-start | bytes 32768 | tf_op jit(solution)/shard_map/all_to_all | solution.py:19
  75.3 135.7 %all-reduce.5.cloned.1.call-start = ((), (), s32[]{:S(2)}) async-start(), calls=%async_computation.3 | async-start | bytes 524288 | tf_op jit(solution)/shard_map/psum | solution.py:115
Sparse Core Ops, SparseCore 0:
  70.3 99.2 all-reduce.2
  172.0 38.9 all-reduce.4
